TPU v7x, 32 devices: a whole 2x2x4 slice. The times are simulated.
32 devices in a mesh: lat: 4 (over z), lon: 8 (over y, x, core).
Axes of the slice: x: 2, y: 2, z: 4, core: 2. Of those that a mesh axis runs over, the one named last changes fastest.
Arguments:
- tracers: float32 [16, 8, 64, 1024], P(None, None, 'lat', 'lon'), may hold values from -6 to 6
- winds: float32 [3, 8, 64, 1024], P(None, None, 'lat', 'lon'), may hold values from -4 to 4
- depart_first: int32 [3, 8, 64, 1024], P(None, None, 'lat', 'lon'), may hold values from -3 to 2, as said below
- depart_second: int32 [3, 8, 64, 1024], P(None, None, 'lat', 'lon'), may hold values from -2 to 1, as said below
- fluxes: bfloat16 [384, 128, 256], P(('lat', 'lon')), may hold values from 0.049804688 to 5
- remap_weights: bfloat16 [384, 4, 256, 128], P(('lat', 'lon')), may hold values from 0.00019931793 to 0.019897461
- target_device: int32 [384, 4], P(('lat', 'lon')), may hold values from 0 to 31, all different within a row; in each aligned block of 12 rows (0 to 11, 12 to 23, ...) at most 2 rows name the same one
- target_block: int32 [384, 4], P(('lat', 'lon')), may hold values from 0 to 15
Outputs:
- advected: float32 [16, 8, 64, 1024], P(None, None, 'lat', 'lon')
Inputs may be any that keep to these rules, and one draw needn't show every extreme that they name: `depart_first`: component 0 (levels) is -1 or 0; components 1 and 2 are row and column offsets. `depart_second`: component 0 (levels) is -1 or 0; components 1 and 2 are row and column offsets. `target_device`: device g is the one at lat index g // 8 and lon index g % 8. Each row names 4 different devices; among the rows of one device no device is named more than 2 times.
All inputs are finite; a program needn't handle non-finite values.
Results may differ from a plain program's by a relative error of at most 0.00088.
Values may be sent and summed in bfloat16 or wider, within the bound.
A program may use at most 192 MiB of HBM per device.

v0:
```python
import jax
import jax.numpy as jnp
from jax import lax
from jax.sharding import PartitionSpec as P

NTR = 16
CAP = 2
BLK_DEV = 16
HMAX = 3


def padded_2(block, sides, width, periodic):
    for axis, dim in sides:
        count = lax.axis_size(axis)
        forward = [(i, i + 1) for i in range(count - 1)]
        if periodic:
            forward.append((count - 1, 0))
        backward = [(target, source) for source, target in forward]
        low = lax.ppermute(
            lax.slice_in_dim(block, block.shape[dim] - width, None, axis=dim), axis, forward
        )
        high = lax.ppermute(lax.slice_in_dim(block, 0, width, axis=dim), axis, backward)
        block = jnp.concatenate([low, block, high], axis=dim)
    return block


def cubic_weights(frac):
    first = -frac * (frac - 1.0) * (frac - 2.0) / 6.0
    second = (frac + 1.0) * (frac - 1.0) * (frac - 2.0) / 2.0
    third = -(frac + 1.0) * frac * (frac - 2.0) / 2.0
    fourth = (frac + 1.0) * frac * (frac - 1.0) / 6.0
    return (first, second, third, fourth)


def offset_weights(offset, frac, reach):
    stencil = cubic_weights(frac)
    spread = []
    for target in range(-reach, reach + 1):
        weight = jnp.zeros(frac.shape, jnp.float32)
        for step in range(4):
            weight = weight + jnp.where(offset + step - 1 == target, stencil[step], 0.0)
        spread.append(weight)
    return spread


def tricubic(padded, depart, frac, margin):
    chans, levels, rows_wide, cols_wide = padded.shape
    rows = rows_wide - 2 * margin
    cols = cols_wide - 2 * margin
    lowest = padded[:, :1]
    highest = padded[:, -1:]
    stacked = jnp.concatenate([lowest, lowest, padded, highest, highest], axis=1)
    level_w = offset_weights(depart[0], frac[0], 2)
    row_w = offset_weights(depart[1], frac[1], margin)
    col_w = offset_weights(depart[2], frac[2], margin)
    total = jnp.zeros((chans, levels, rows, cols), jnp.float32)
    for above in range(5):
        for across in range(2 * margin + 1):
            inner = jnp.zeros((chans, levels, rows, cols), jnp.float32)
            for sideways in range(2 * margin + 1):
                piece = stacked[
                    :, above : above + levels, across : across + rows, sideways : sideways + cols
                ]
                inner = inner + col_w[sideways][None] * piece
            total = total + (level_w[above] * row_w[across])[None] * inner
    return total


def body(
    tracers, winds, depart_first, depart_second, fluxes, remap_weights, target_device, target_block
):
    wide = HMAX + 1
    narrow = max((HMAX + 1) // 2 + 1, HMAX // 2 + 2)
    wind_side = padded_2(winds, (("lon", 3),), wide, True)
    wind_wide = padded_2(wind_side, (("lat", 2),), wide, False)
    tracer_side = padded_2(tracers, (("lon", 3),), narrow, True)
    tracer_wide = padded_2(tracer_side, (("lat", 2),), narrow, False)
    shape = winds.shape[1:]
    frac_first = jnp.clip(-winds - depart_first.astype(jnp.float32), 0.0, 1.0)
    midwind = tricubic(wind_wide, depart_first, frac_first, wide)
    frac_second = jnp.clip(-(winds + midwind) * 0.5 - depart_second.astype(jnp.float32), 0.0, 1.0)
    moved = tricubic(tracer_wide, depart_second, frac_second, narrow)
    tiles, links = target_device.shape
    rows_count, block_cols = (fluxes.shape[1], remap_weights.shape[3])
    items = tiles * links
    remapped = jnp.einsum(
        "trc,tkcb->tkrb", fluxes, remap_weights, preferred_element_type=jnp.float32
    )
    remapped = remapped.astype(jnp.bfloat16).reshape(items, rows_count, block_cols)
    lat_count = lax.axis_size("lat")
    lon_count = lax.axis_size("lon")
    devices = lat_count * lon_count
    slot_count = devices * CAP
    owners = target_device.reshape(items)
    item_iota = lax.broadcasted_iota(jnp.int32, (items, items), 1)
    item_rows = lax.broadcasted_iota(jnp.int32, (items, items), 0)
    earlier = jnp.logical_and(owners[:, None] == owners[None, :], item_iota < item_rows)
    rank = jnp.sum(earlier.astype(jnp.int32), axis=1)
    slot = owners * CAP + rank
    slot_iota = lax.broadcasted_iota(jnp.int32, (slot_count, items), 0)
    hit = slot[None, :] == slot_iota
    present = jnp.any(hit, axis=1)
    source_item = jnp.sum(
        jnp.where(hit, lax.broadcasted_iota(jnp.int32, (slot_count, items), 1), 0), axis=1
    )
    outgoing = jnp.take(remapped, source_item, axis=0)
    outgoing = jnp.where(present[:, None, None], outgoing, jnp.zeros_like(outgoing))
    labels = jnp.where(present, jnp.take(target_block.reshape(items), source_item), -1)
    data = outgoing.reshape(devices, CAP, rows_count, block_cols)
    marks = labels.reshape(devices, CAP)
    arrived, arrived_labels = (
        lax.all_to_all(data, ("lat", "lon"), split_axis=0, concat_axis=0, tiled=True),
        lax.all_to_all(marks, ("lat", "lon"), split_axis=0, concat_axis=0, tiled=True),
    )
    arrived_flat = arrived.reshape(slot_count, rows_count * block_cols)
    block_iota = lax.broadcasted_iota(jnp.int32, (BLK_DEV, slot_count), 0)
    selector = (arrived_labels.reshape(1, slot_count) == block_iota).astype(jnp.bfloat16)
    blocks = jnp.dot(selector, arrived_flat, preferred_element_type=jnp.float32)
    levels, lat_rows, lon_cols = shape
    grid = blocks.reshape(BLK_DEV, NTR, levels, block_cols).transpose(1, 2, 0, 3)
    return moved + grid


def solution(mesh):
    in_specs = (
        P(None, None, "lat", "lon"),
        P(None, None, "lat", "lon"),
        P(None, None, "lat", "lon"),
        P(None, None, "lat", "lon"),
        P(("lat", "lon"), None, None),
        P(("lat", "lon"), None, None, None),
        P(("lat", "lon"), None),
        P(("lat", "lon"), None),
    )
    out_specs = P(None, None, "lat", "lon")
    return jax.shard_map(body, mesh=mesh, in_specs=in_specs, out_specs=out_specs, check_vma=False)
```

profile of v0, /device:TPU:10, one launch (start us, length us, event | category | flops | bytes accessed | tf_op | source)
XLA Modules:
  0.0 473.4 jit_solution(3937024502456102660)
XLA Ops:
  0.0 2.0 fusion.806
  3.7 3.2 fusion.805
  6.9 2.7 copy.44
  9.7 2.7 copy.45
  20.5 6.9 %all-to-all-start = ((s32[32,1,2]{2,1,0:T(1,128)}), s32[32,1,2]{2,1,0:T(1,128)}, u32[]{:S(2)}, u32[]{:S(2)}) async-start(s32[32,1,2]{2,1,0:T(1,128)} %bitcast.235), calls=%async_computation | async-start | bytes 32768 | tf_op jit(solution)/shard_map/all_to_all | solution.py:113
  32.3 1.9 multiply_bitcast_fusion.70
  34.2 2.1 multiply_bitcast_fusion.51
  37.0 2.1 multiply_bitcast_fusion.77
  39.0 2.3 convolution_convert_fusion
  41.3 3.6 gather_fusion.1
  45.0 3.4 copy.39
  52.4 5.9 %all-to-all-start.1 = ((bf16[32,2,128,128]{3,2,1,0:T(8,128)(2,1)}), bf16[32,2,128,128]{3,2,1,0:T(8,128)(2,1)}, u32[]{:S(2)}, u32[]{:S(2)}) async-start(bf16[32,2,128,128]{3,2,1,0:T(8,128)(2,1)} %select_select_fusion), calls=%async_computation.1 | async-start | bytes 4194304 | tf_op jit(solution)/shard_map/all_to_all | solution.py:112
  60.3 1.8 pad_maximum_fusion.19
  62.2 3.4 collective-permute-start.2
  65.5 3.1 collective-permute-start.3
  70.4 2.0 copy.32
  72.4 1.8 pad_maximum_fusion.10
  74.3 2.7 collective-permute-start.6
  77.0 3.4 collective-permute-start.7
  80.5 26.3 %collective-permute-done.2 = f32[3,8,4,136]{3,2,1,0:T(4,128)} collective-permute-done((f32[3,8,4,136]{3,2,1,0:T(4,128)}, f32[3,8,4,136]{3,2,1,0:T(4,128)}, u32[]{:S(2)}, u32[]{:S(2)}) %collective-permute-start.2) | collective-permute-done | bytes 52256 | tf_op jit(solution)/shard_map/ppermute | solution.py:19
  106.8 1.9 collective-permute-done.3
  120.5 1.8 maximum_maximum_fusion.4
  139.4 10.7 %fusion.542 = f32[3,8,16,128]{3,2,1,0:T(8,128)} fusion(f32[3,8,16,128]{3,2,1,0:T(8,128)} %mul.6969, f32[3,8,16,128]{3,2,1,0:T(8,128)} %mul.6704, f32[3,8,20,136]{3,2,1,0:T(8,128)S(1)} %get-tuple-element.72, f32[3,8,16,128]{3,2,1,0:T(8,128)S(1)} %mul.6701, f32[3,8,16,128]{3,2,1,0:T(8,128)S(1)} %mul.6698, f32[3,8,16,128]{3,2,1,0:T(8,128)S(1)} %mul.6695, ...), kind=kLoop, calls=%fused_computation.1022 | loop fusion | flops 18677760 | bytes 41484288 | tf_op jit(solution)/shard_map/add | solution.py:65
  180.6 10.5 %fusion.333 = f32[3,8,16,128]{3,2,1,0:T(8,128)S(1)} fusion(f32[3,8,16,128]{3,2,1,0:T(8,128)} %max.8, f32[3,8,16,128]{3,2,1,0:T(8,128)} %min.12, f32[3,8,16,128]{3,2,1,0:T(8,128)} %convert_element_type.17, f32[3,8,16,128]{3,2,1,0:T(8,128)} %mul.7279, f32[3,8,16,128]{3,2,1,0:T(8,128)S(1)} %copy-done.9, f32[3,8,16,128]{3,2,1,0:T(8,128)} %mul.7268, ...), kind=kLoop, calls=%fused_computation.610 | loop fusion | flops 19365888 | bytes 43653120 | tf_op jit(solution)/shard_map/jit(clip)/min | solution.py:81
  195.7 4.5 maximum_maximum_fusion.1
  200.2 4.2 maximum_maximum_fusion.2
  204.4 2.2 fusion.207
  206.7 13.4 %maximum_maximum_fusion = (f32[16,10,22,134]{3,2,1,0:T(8,128)}, f32[16,10,22,134]{3,2,1,0:T(8,128)}) fusion(f32[16,8,3,134]{3,2,1,0:T(4,128)S(1)} %collective-permute-done.7, f32[16,8,16,3]{3,2,1,0:T(8,128)S(1)} %copy-done.8, f32[16,8,16,128]{3,2,1,0:T(8,128)S(1)} %copy-done.4, f32[16,8,16,3]{3,2,1,0:T(8,128)S(1)} %copy-done.6, ...), kind=kLoop, calls=%fused_computation.2 | loop fusion | flops 5660160 | bytes 5660160 | tf_op jit(solution)/shard_map/concatenate | solution.py:52
  220.0 85.8 %fusion.212 = f32[16,8,16,128]{3,2,1,0:T(8,128)} fusion(f32[16,9,22,134]{3,2,1,0:T(8,128)} %copy-done.2, f32[16,10,22,134]{3,2,1,0:T(8,128)} %get-tuple-element.53, f32[8,16,128]{2,1,0:T(8,128)} %get-tuple-element.159, f32[8,16,128]{2,1,0:T(8,128)} %get-tuple-element.151, f32[8,16,128]{2,1,0:T(8,128)} %get-tuple-element.143, ...), kind=kLoop, calls=%fused_computation.391 | loop fusion | flops 42991616 | bytes 82968576 | tf_op jit(solution)/shard_map/add | solution.py:65
  305.9 3.0 copy.56
  308.8 1.9 copy.47
  310.8 162.4 %fusion.5 = f32[16,8,16,128]{3,2,1,0:T(8,128)} fusion(bf16[16,8,128,64]{2,1,0,3:T(8,128)(2,1)} %bitcast.234, f32[16,8,16,128]{3,2,1,0:T(8,128)} %param.8, f32[16,8,16,3]{3,2,1,0:T(8,128)} %copy-done.7, f32[16,8,16,128]{3,2,1,0:T(8,128)} %get-tuple-element.139, f32[16,8,16,3]{3,2,1,0:T(8,128)} %copy-done.5, f32[16,10,22,134]{3,2,1,0:T(8,128)} %get-tuple-element.54, ...), kind=kOutput, calls=%fused_computation.22 | convolution fusion | flops 127665152 | bytes 174047488 | tf_op jit(solution)/shard_map/dot_general | solution.py:118
  (280 shorter events, 86.4 us)
Async XLA Ops:
  0.0 39.0 %copy-start = (bf16[12,4,256,128]{3,2,1,0:T(8,128)(2,1)S(1)}, bf16[12,4,256,128]{3,2,1,0:T(8,128)(2,1)}, u32[]{:S(2)}) copy-start(bf16[12,4,256,128]{3,2,1,0:T(8,128)(2,1)} %param.13) | copy-start | bytes 9437188
  2.0 58.3 %collective-permute-start = (f32[3,8,16,4]{3,2,1,0:T(8,128)}, f32[3,8,16,4]{3,2,1,0:T(8,128)S(1)}, u32[]{:S(2)}, u32[]{:S(2)}) collective-permute-start(f32[3,8,16,4]{3,2,1,0:T(8,128)} %get-tuple-element.134), channel_id=1, source_target_pairs={{0,1},{1,2},{2,3},{3,4},{4,5},{5,6},{6,7},{7,0},{8,9},{9,10},{10,1... | collective-permute-start | bytes 18440 | tf_op jit(solution)/shard_map/ppermute | solution.py:19
  2.0 58.3 %collective-permute-start.1 = (f32[3,8,16,4]{3,2,1,0:T(8,128)}, f32[3,8,16,4]{3,2,1,0:T(8,128)}, u32[]{:S(2)}, u32[]{:S(2)}) collective-permute-start(f32[3,8,16,4]{3,2,1,0:T(8,128)} %get-tuple-element.135), channel_id=1, source_target_pairs={{1,0},{2,1},{3,2},{4,3},{5,4},{6,5},{7,6},{0,7},{9,8},{10,9},{11,1... | collective-permute-start | bytes 18440 | tf_op jit(solution)/shard_map/ppermute | solution.py:22
  9.7 58.9 %collective-permute-start.4 = (f32[16,8,16,3]{2,1,3,0:T(8,128)}, f32[16,8,16,3]{2,1,3,0:T(8,128)}, u32[]{:S(2)}, u32[]{:S(2)}) collective-permute-start(f32[16,8,16,3]{2,1,3,0:T(8,128)} %copy.44), channel_id=1, source_target_pairs={{0,1},{1,2},{2,3},{3,4},{4,5},{5,6},{6,7},{7,0},{8,9},{9,10},{10,1... | collective-permute-start | bytes 73736 | tf_op jit(solution)/shard_map/ppermute | solution.py:19
  12.4 58.0 %collective-permute-start.5 = (f32[16,8,16,3]{2,1,3,0:T(8,128)}, f32[16,8,16,3]{2,1,3,0:T(8,128)}, u32[]{:S(2)}, u32[]{:S(2)}) collective-permute-start(f32[16,8,16,3]{2,1,3,0:T(8,128)} %copy.45), channel_id=1, source_target_pairs={{1,0},{2,1},{3,2},{4,3},{5,4},{6,5},{7,6},{0,7},{9,8},{10,9},{11,1... | collective-permute-start | bytes 73736 | tf_op jit(solution)/shard_map/ppermute | solution.py:22
  20.5 31.8 %all-to-all-start = ((s32[32,1,2]{2,1,0:T(1,128)}), s32[32,1,2]{2,1,0:T(1,128)}, u32[]{:S(2)}, u32[]{:S(2)}) async-start(s32[32,1,2]{2,1,0:T(1,128)} %bitcast.235), calls=%async_computation | async-start | bytes 32768 | tf_op jit(solution)/shard_map/all_to_all | solution.py:113
  52.4 253.5 %all-to-all-start.1 = ((bf16[32,2,128,128]{3,2,1,0:T(8,128)(2,1)}), bf16[32,2,128,128]{3,2,1,0:T(8,128)(2,1)}, u32[]{:S(2)}, u32[]{:S(2)}) async-start(bf16[32,2,128,128]{3,2,1,0:T(8,128)(2,1)} %select_select_fusion), calls=%async_computation.1 | async-start | bytes 4194304 | tf_op jit(solution)/shard_map/all_to_all | solution.py:112
  62.2 44.6 %collective-permute-start.2 = (f32[3,8,4,136]{3,2,1,0:T(4,128)}, f32[3,8,4,136]{3,2,1,0:T(4,128)}, u32[]{:S(2)}, u32[]{:S(2)}) collective-permute-start(f32[3,8,4,136]{3,2,1,0:T(4,128)} %get-tuple-element.73), channel_id=1, source_target_pairs={{0,8},{8,16},{16,24},{1,9},{9,17},{17,25},{2,10},{10,18},{18,26},{... | collective-permute-start | bytes 156680 | tf_op jit(solution)/shard_map/ppermute | solution.py:19
  65.5 43.1 %collective-permute-start.3 = (f32[3,8,4,136]{3,2,1,0:T(4,128)}, f32[3,8,4,136]{3,2,1,0:T(4,128)}, u32[]{:S(2)}, u32[]{:S(2)}) collective-permute-start(f32[3,8,4,136]{3,2,1,0:T(4,128)} %get-tuple-element.74), channel_id=1, source_target_pairs={{8,0},{16,8},{24,16},{9,1},{17,9},{25,17},{10,2},{18,10},{26,18},{... | collective-permute-start | bytes 156680 | tf_op jit(solution)/shard_map/ppermute | solution.py:22
  70.4 36.4 %copy-start.5 = (f32[16,8,16,3]{3,2,1,0:T(8,128)}, f32[16,8,16,3]{3,2,1,0:T(8,128)S(1)}, u32[]{:S(2)}) copy-start(f32[16,8,16,3]{3,2,1,0:T(8,128)S(1)} %copy.31) | copy-start | bytes 73732
  72.3 34.4 %copy-start.7 = (f32[16,8,16,3]{3,2,1,0:T(8,128)}, f32[16,8,16,3]{3,2,1,0:T(8,128)S(1)}, u32[]{:S(2)}) copy-start(f32[16,8,16,3]{3,2,1,0:T(8,128)S(1)} %copy.32) | copy-start | bytes 73732
  72.3 37.9 %copy-start.10 = (f32[8,16,128]{2,1,0:T(8,128)S(1)}, f32[8,16,128]{2,1,0:T(8,128)}, u32[]{:S(2)}) copy-start(f32[8,16,128]{2,1,0:T(8,128)} %get-tuple-element.119) | copy-start | bytes 196612
  72.3 37.9 %copy-start.11 = (f32[8,16,128]{2,1,0:T(8,128)S(1)}, f32[8,16,128]{2,1,0:T(8,128)}, u32[]{:S(2)}) copy-start(f32[8,16,128]{2,1,0:T(8,128)} %get-tuple-element.118) | copy-start | bytes 196612
  72.4 37.9 %copy-start.12 = (f32[8,16,128]{2,1,0:T(8,128)S(1)}, f32[8,16,128]{2,1,0:T(8,128)}, u32[]{:S(2)}) copy-start(f32[8,16,128]{2,1,0:T(8,128)} %get-tuple-element.117) | copy-start | bytes 196612
  72.4 37.9 %copy-start.13 = (f32[8,16,128]{2,1,0:T(8,128)S(1)}, f32[8,16,128]{2,1,0:T(8,128)}, u32[]{:S(2)}) copy-start(f32[8,16,128]{2,1,0:T(8,128)} %get-tuple-element.124) | copy-start | bytes 196612
  72.4 37.9 %copy-start.14 = (f32[8,16,128]{2,1,0:T(8,128)S(1)}, f32[8,16,128]{2,1,0:T(8,128)}, u32[]{:S(2)}) copy-start(f32[8,16,128]{2,1,0:T(8,128)} %get-tuple-element.116) | copy-start | bytes 196612
  72.4 37.9 %copy-start.15 = (f32[8,16,128]{2,1,0:T(8,128)S(1)}, f32[8,16,128]{2,1,0:T(8,128)}, u32[]{:S(2)}) copy-start(f32[8,16,128]{2,1,0:T(8,128)} %get-tuple-element.115) | copy-start | bytes 196612
  72.4 37.9 %copy-start.16 = (f32[8,16,128]{2,1,0:T(8,128)S(1)}, f32[8,16,128]{2,1,0:T(8,128)}, u32[]{:S(2)}) copy-start(f32[8,16,128]{2,1,0:T(8,128)} %get-tuple-element.114) | copy-start | bytes 196612
  72.4 37.9 %copy-start.17 = (f32[8,16,128]{2,1,0:T(8,128)S(1)}, f32[8,16,128]{2,1,0:T(8,128)}, u32[]{:S(2)}) copy-start(f32[8,16,128]{2,1,0:T(8,128)} %get-tuple-element.113) | copy-start | bytes 196612
  74.3 121.0 %collective-permute-start.6 = (f32[16,8,3,134]{3,2,1,0:T(4,128)}, f32[16,8,3,134]{3,2,1,0:T(4,128)S(1)}, u32[]{:S(2)}, u32[]{:S(2)}) collective-permute-start(f32[16,8,3,134]{3,2,1,0:T(4,128)} %get-tuple-element.61), channel_id=1, source_target_pairs={{0,8},{8,16},{16,24},{1,9},{9,17},{17,25},{2,10},{10,18},{18,26},{... | collective-permute-start | bytes 617480 | tf_op jit(solution)/shard_map/ppermute | solution.py:19
  77.0 118.3 %collective-permute-start.7 = (f32[16,8,3,134]{3,2,1,0:T(4,128)}, f32[16,8,3,134]{3,2,1,0:T(4,128)S(1)}, u32[]{:S(2)}, u32[]{:S(2)}) collective-permute-start(f32[16,8,3,134]{3,2,1,0:T(4,128)} %get-tuple-element.62), channel_id=1, source_target_pairs={{8,0},{16,8},{24,16},{9,1},{17,9},{25,17},{10,2},{18,10},{26,18},{... | collective-permute-start | bytes 617480 | tf_op jit(solution)/shard_map/ppermute | solution.py:22
  150.3 30.3 %copy-start.24 = (f32[3,8,16,128]{3,2,1,0:T(8,128)S(1)}, f32[3,8,16,128]{3,2,1,0:T(8,128)}, u32[]{:S(2)}) copy-start(f32[3,8,16,128]{3,2,1,0:T(8,128)} %mul.6689) | copy-start | bytes 589828
  150.3 30.3 %copy-start.25 = (f32[3,8,16,128]{3,2,1,0:T(8,128)S(1)}, f32[3,8,16,128]{3,2,1,0:T(8,128)}, u32[]{:S(2)}) copy-start(f32[3,8,16,128]{3,2,1,0:T(8,128)} %mul.6692) | copy-start | bytes 589828
  150.3 30.3 %copy-start.26 = (f32[3,8,16,128]{3,2,1,0:T(8,128)S(1)}, f32[3,8,16,128]{3,2,1,0:T(8,128)}, u32[]{:S(2)}) copy-start(f32[3,8,16,128]{3,2,1,0:T(8,128)} %mul.6704) | copy-start | bytes 589828
  150.3 30.3 %copy-start.27 = (f32[3,8,16,128]{3,2,1,0:T(8,128)S(1)}, f32[3,8,16,128]{3,2,1,0:T(8,128)}, u32[]{:S(2)}) copy-start(f32[3,8,16,128]{3,2,1,0:T(8,128)} %mul.6680) | copy-start | bytes 589828
  150.3 30.2 %copy-start.31 = (f32[3,8,16,128]{3,2,1,0:T(8,128)S(1)}, f32[3,8,16,128]{3,2,1,0:T(8,128)}, u32[]{:S(2)}) copy-start(f32[3,8,16,128]{3,2,1,0:T(8,128)} %fusion.542) | copy-start | bytes 589828
  150.3 30.2 %copy-start.32 = (f32[3,8,16,128]{3,2,1,0:T(8,128)S(1)}, f32[3,8,16,128]{3,2,1,0:T(8,128)}, u32[]{:S(2)}) copy-start(f32[3,8,16,128]{3,2,1,0:T(8,128)} %fusion.514) | copy-start | bytes 589828
  150.3 30.2 %copy-start.33 = (f32[3,8,16,128]{3,2,1,0:T(8,128)S(1)}, f32[3,8,16,128]{3,2,1,0:T(8,128)}, u32[]{:S(2)}) copy-start(f32[3,8,16,128]{3,2,1,0:T(8,128)} %fusion.523) | copy-start | bytes 589828
  150.3 30.2 %copy-start.34 = (f32[3,8,16,128]{3,2,1,0:T(8,128)S(1)}, f32[3,8,16,128]{3,2,1,0:T(8,128)}, u32[]{:S(2)}) copy-start(f32[3,8,16,128]{3,2,1,0:T(8,128)} %get-tuple-element.131) | copy-start | bytes 589828
  150.3 30.2 %copy-start.21 = (f32[3,8,16,128]{3,2,1,0:T(8,128)S(1)}, f32[3,8,16,128]{3,2,1,0:T(8,128)}, u32[]{:S(2)}) copy-start(f32[3,8,16,128]{3,2,1,0:T(8,128)} %copy-done.20) | copy-start | bytes 589828
  150.3 30.2 %copy-start.23 = (f32[3,8,16,128]{3,2,1,0:T(8,128)S(1)}, f32[3,8,16,128]{3,2,1,0:T(8,128)}, u32[]{:S(2)}) copy-start(f32[3,8,16,128]{3,2,1,0:T(8,128)} %copy-done.22) | copy-start | bytes 589828
  310.8 162.5 %copy-start.1 = (bf16[12,4,256,128]{3,2,1,0:T(8,128)(2,1)S(1)}, bf16[12,4,256,128]{3,2,1,0:T(8,128)(2,1)}, u32[]{:S(2)}) copy-start(bf16[12,4,256,128]{3,2,1,0:T(8,128)(2,1)} %param.13) | copy-start | bytes 9437188
  (64 other events, 642.3 us)
where the time goes:
time: 478 us; the launch traced here: 473 us
  other arithmetic  168 us (35%)
  matrix products  165 us (35%)
  local copies, waits for them, and re-layouts  82 us (17%)
  starting transfers between devices  28.9 us (6%)
  waiting for transfers between devices  28.2 us (6%)
    dot_general x1, matrix products, body(): blocks = jnp.dot(selector, arrived_flat, preferred_element_type=jnp.float32)  162 us
    add x3, other arithmetic, tricubic(): total = total + (level_w[above] * row_w[across])[None] * inner  98.1 us
    mul x43, local copies, waits for them, and re-layouts, tricubic(): total = total + (level_w[above] * row_w[across])[None] * inner  42.1 us
    ppermute x4, waiting for transfers between devices, padded_2(): lax.ppermute(lax.slice_in_dim(block, block.shape[dim] - width, None, axis...  26.3 us
    concatenate x4, other arithmetic, tricubic(): jnp.concatenate([lowest, lowest, padded, highest, highest], axis=1)  21.4 us
    mul x9, other arithmetic, tricubic(): total = total + (level_w[above] * row_w[across])[None] * inner  13.3 us
    unnamed x178, local copies, waits for them, and re-layouts  12.2 us
    min x1, other arithmetic, body(): jnp.clip(-(winds + midwind) * 0.5 - depart_second.astype(jnp.float32), 0....  10.5 us
  transfers between devices with their start and end apart: 10, of which 2 were waited for; matrix products, arithmetic and copies ran while one was open for 52% of the time, Pallas kernels for 0%

commit v1 on v0

--- a/solution.py
+++ b/solution.py
@@ -1,6 +1,10 @@
+import functools
+
 import jax
 import jax.numpy as jnp
 from jax import lax
+from jax.experimental import pallas as pl
+from jax.experimental.pallas import tpu as pltpu
 from jax.sharding import PartitionSpec as P
 
 NTR = 16
@@ -32,38 +36,193 @@
     return (first, second, third, fourth)
 
 
+def level_weights(offset, frac):
+    s0, s1, s2, s3 = cubic_weights(frac)
+    down = offset < 0
+    zero = jnp.zeros_like(frac)
+    return [
+        jnp.where(down, s0, zero),
+        jnp.where(down, s1, s0),
+        jnp.where(down, s2, s1),
+        jnp.where(down, s3, s2),
+        jnp.where(down, zero, s3),
+    ]
+
+
 def offset_weights(offset, frac, reach):
     stencil = cubic_weights(frac)
     spread = []
     for target in range(-reach, reach + 1):
         weight = jnp.zeros(frac.shape, jnp.float32)
         for step in range(4):
-            weight = weight + jnp.where(offset + step - 1 == target, stencil[step], 0.0)
+            weight = jnp.where(offset == target - step + 1, stencil[step], weight)
         spread.append(weight)
     return spread
 
 
-def tricubic(padded, depart, frac, margin):
-    chans, levels, rows_wide, cols_wide = padded.shape
-    rows = rows_wide - 2 * margin
-    cols = cols_wide - 2 * margin
-    lowest = padded[:, :1]
-    highest = padded[:, -1:]
-    stacked = jnp.concatenate([lowest, lowest, padded, highest, highest], axis=1)
-    level_w = offset_weights(depart[0], frac[0], 2)
-    row_w = offset_weights(depart[1], frac[1], margin)
-    col_w = offset_weights(depart[2], frac[2], margin)
-    total = jnp.zeros((chans, levels, rows, cols), jnp.float32)
-    for above in range(5):
-        for across in range(2 * margin + 1):
-            inner = jnp.zeros((chans, levels, rows, cols), jnp.float32)
-            for sideways in range(2 * margin + 1):
-                piece = stacked[
-                    :, above : above + levels, across : across + rows, sideways : sideways + cols
-                ]
-                inner = inner + col_w[sideways][None] * piece
-            total = total + (level_w[above] * row_w[across])[None] * inner
-    return total
+def advect_kernel(
+    wide, narrow, winds_ref, first_ref, second_ref, wpad_ref, main_ref, halo_ref, out_ref,
+    shifted, lhs, rhs, mid_ref, lev_w, row_w, col_w, col_at
+):
+    levels, height, chans, lanes = main_ref.shape
+    comps, rows = winds_ref.shape[0], winds_ref.shape[1]
+    taps, reach = 2 * wide + 1, 2 * narrow + 1
+
+    def shift_row(r, carry):
+        for comp in range(comps):
+            row = wpad_ref[comp, r]
+            for e in range(taps):
+                piece = row[:, e : e + lanes]
+                low, high = piece[:1], piece[levels - 1 :]
+                shifted[e * 5 + 0, comp, r] = jnp.concatenate([low, low, piece[: levels - 2]], axis=0)
+                shifted[e * 5 + 1, comp, r] = jnp.concatenate([low, piece[: levels - 1]], axis=0)
+                shifted[e * 5 + 2, comp, r] = piece
+                shifted[e * 5 + 3, comp, r] = jnp.concatenate([piece[1:], high], axis=0)
+                shifted[e * 5 + 4, comp, r] = jnp.concatenate([piece[2:], high, high], axis=0)
+        return carry
+
+    lax.fori_loop(0, wpad_ref.shape[1], shift_row, 0)
+
+    def wind_row(i, carry):
+        wind = [winds_ref[comp, i] for comp in range(comps)]
+        off = [first_ref[comp, i] for comp in range(comps)]
+        frac = [
+            jnp.clip(-wind[comp] - off[comp].astype(jnp.float32), 0.0, 1.0) for comp in range(comps)
+        ]
+        lw = level_weights(off[0], frac[0])
+        rw = offset_weights(off[1], frac[1], wide)
+        cw = offset_weights(off[2], frac[2], wide)
+        total = [jnp.zeros((levels, lanes), jnp.float32) for comp in range(comps)]
+        for across in range(taps):
+            for above in range(5):
+                pair = lw[above] * rw[across]
+                for comp in range(comps):
+                    inner = cw[0] * shifted[above, comp, i + across]
+                    for e in range(1, taps):
+                        inner = inner + cw[e] * shifted[e * 5 + above, comp, i + across]
+                    total[comp] = total[comp] + pair * inner
+        off = [second_ref[comp, i] for comp in range(comps)]
+        frac = [
+            jnp.clip(
+                -(wind[comp] + total[comp]) * 0.5 - off[comp].astype(jnp.float32), 0.0, 1.0
+            )
+            for comp in range(comps)
+        ]
+        for n, weight in enumerate(level_weights(off[0], frac[0])):
+            lev_w[n, i] = weight
+        for n, weight in enumerate(offset_weights(off[1], frac[1], narrow)):
+            row_w[n, i] = weight
+        for n, weight in enumerate(cubic_weights(frac[2])):
+            col_w[n, i] = weight
+        col_at[i] = off[2] - 1 + lax.broadcasted_iota(jnp.int32, (levels, lanes), 1)
+        return carry
+
+    lax.fori_loop(0, rows, wind_row, 0)
+
+    lane = lax.broadcasted_iota(jnp.int32, (chans, lanes), 1)
+    is_low = jnp.logical_and(lane >= 8, lane < 16)
+
+    def split_row(r, carry):
+        for level in range(levels + 4):
+            at = min(max(level - 2, 0), levels - 1)
+            value = main_ref[at, r]
+            top = value.astype(jnp.bfloat16)
+            rest = (value - top.astype(jnp.float32)).astype(jnp.bfloat16)
+            edge = halo_ref[at, r]
+            edge_top = edge.astype(jnp.bfloat16).astype(jnp.float32)
+            edge = jnp.where(is_low, edge - edge_top, edge_top).astype(jnp.bfloat16)
+            lhs[level, r, :, 0:lanes] = top
+            lhs[level, r, :, lanes : 2 * lanes] = rest
+            lhs[level, r, :, 2 * lanes : 3 * lanes] = top
+            lhs[level, r, :, 3 * lanes : 4 * lanes] = edge
+        return carry
+
+    lax.fori_loop(0, height, split_row, 0)
+
+    rhs[...] = jnp.zeros_like(rhs)
+    inside = lax.broadcasted_iota(jnp.int32, (lanes, lanes), 0)
+    spot = lax.broadcasted_iota(jnp.int32, (8, lanes), 0)
+    outside = jnp.where(spot < 4, spot - 4, spot + (lanes - 4))
+
+    def step(t, carry):
+        level, first_row = t // (rows // 2), (t % (rows // 2)) * 2
+        for side in range(2):
+            i = first_row + side
+            at = col_at[i, pl.ds(level, 1), :]
+            weights = [col_w[n, i, pl.ds(level, 1), :] for n in range(4)]
+            cols = slice(side * lanes, (side + 1) * lanes)
+
+            def spread(where):
+                away = where - at
+                value = jnp.where(away == 0, weights[0], 0.0)
+                for n in range(1, 4):
+                    value = jnp.where(away == n, weights[n], value)
+                top = value.astype(jnp.bfloat16).astype(jnp.float32)
+                return top, value - top
+
+            top, rest = spread(inside)
+            top16 = top.astype(jnp.bfloat16)
+            rhs[0:lanes, cols] = top16
+            rhs[lanes : 2 * lanes, cols] = top16
+            rhs[2 * lanes : 3 * lanes, cols] = rest.astype(jnp.bfloat16)
+            top, rest = spread(outside)
+            rhs[3 * lanes : 3 * lanes + 32, cols] = jnp.concatenate(
+                [top, top, rest, jnp.zeros_like(rest)], axis=0
+            ).astype(jnp.bfloat16)
+        span = reach + 1
+        left = lhs[pl.ds(level, 5), pl.ds(first_row, span)].reshape(5 * span * chans, 4 * lanes)
+        done = jnp.dot(left, rhs[...], preferred_element_type=jnp.float32)
+        for side in range(2):
+            i = first_row + side
+            cols = slice(side * lanes, (side + 1) * lanes)
+            rw = [row_w[n, i, pl.ds(level, 1), :] for n in range(reach)]
+            total = jnp.zeros((chans, lanes), jnp.float32)
+            for above in range(5):
+                lw = lev_w[above, i, pl.ds(level, 1), :]
+                inner = jnp.zeros((chans, lanes), jnp.float32)
+                for n in range(reach):
+                    start = (above * span + n + side) * chans
+                    inner = inner + rw[n] * done[start : start + chans, cols]
+                total = total + lw * inner
+            out_ref[level, i] = total
+        return carry
+
+    lax.fori_loop(0, levels * (rows // 2), step, 0)
+
+
+def advect(winds, depart_first, depart_second, wind_wide, tracer_wide, wide, narrow):
+    chans, levels, height, _ = tracer_wide.shape
+    comps, _, rows, lanes = winds.shape
+    by_row = lambda array: array.transpose(0, 2, 1, 3)
+    turned = tracer_wide.transpose(1, 2, 0, 3)
+    main = turned[..., narrow : narrow + lanes]
+    edge = jnp.concatenate([turned[..., :narrow], turned[..., narrow + lanes :]], axis=3)
+    gap = jnp.zeros(edge.shape[:3] + (4 - narrow,), jnp.float32)
+    edge = jnp.concatenate([gap, edge, gap], axis=3)
+    halo = jnp.concatenate(
+        [edge, edge, edge, jnp.zeros(edge.shape[:3] + (lanes - 24,), jnp.float32)], axis=3
+    )
+    vmem = pl.BlockSpec(memory_space=pltpu.VMEM)
+    moved = pl.pallas_call(
+        functools.partial(advect_kernel, wide, narrow),
+        out_shape=jax.ShapeDtypeStruct((levels, rows, chans, lanes), jnp.float32),
+        in_specs=[vmem] * 6,
+        out_specs=vmem,
+        scratch_shapes=[
+            pltpu.VMEM((5 * (2 * wide + 1), comps, rows + 2 * wide, levels, lanes), jnp.float32),
+            pltpu.VMEM((levels + 4, height, chans, 4 * lanes), jnp.bfloat16),
+            pltpu.VMEM((4 * lanes, 2 * lanes), jnp.bfloat16),
+            pltpu.VMEM((comps, rows, levels, lanes), jnp.float32),
+            pltpu.VMEM((5, rows, levels, lanes), jnp.float32),
+            pltpu.VMEM((2 * narrow + 1, rows, levels, lanes), jnp.float32),
+            pltpu.VMEM((4, rows, levels, lanes), jnp.float32),
+            pltpu.VMEM((rows, levels, lanes), jnp.int32),
+        ],
+        compiler_params=pltpu.CompilerParams(vmem_limit_bytes=48 * 1024 * 1024),
+        cost_estimate=pl.CostEstimate(flops=10**10, bytes_accessed=10**7, transcendentals=0),
+        name="advect",
+    )(by_row(winds), by_row(depart_first), by_row(depart_second), by_row(wind_wide), main, halo)
+    return moved.transpose(2, 0, 1, 3)
 
 
 def body(
@@ -76,10 +235,7 @@
     tracer_side = padded_2(tracers, (("lon", 3),), narrow, True)
     tracer_wide = padded_2(tracer_side, (("lat", 2),), narrow, False)
     shape = winds.shape[1:]
-    frac_first = jnp.clip(-winds - depart_first.astype(jnp.float32), 0.0, 1.0)
-    midwind = tricubic(wind_wide, depart_first, frac_first, wide)
-    frac_second = jnp.clip(-(winds + midwind) * 0.5 - depart_second.astype(jnp.float32), 0.0, 1.0)
-    moved = tricubic(tracer_wide, depart_second, frac_second, narrow)
+    moved = advect(winds, depart_first, depart_second, wind_wide, tracer_wide, wide, narrow)
     tiles, links = target_device.shape
     rows_count, block_cols = (fluxes.shape[1], remap_weights.shape[3])
     items = tiles * links

time: 478 us -> 171 us (0.36)
  matrix products: 165 us -> 4.62 us
  other arithmetic: 168 us -> 15.2 us
  Pallas kernels: 0 us -> 44.4 us
  local copies, waits for them, and re-layouts: 82 us -> 61.4 us
  waiting for transfers between devices: 28.2 us -> 14.5 us
    dot_general x1, matrix products: 162 us -> 1.23 us  [body(): blocks = jnp.dot(selector, arrived_flat, preferred_element_type=jnp.float32)]
    add x6 -> x1, other arithmetic: 103 us -> 0.62 us  [body(): return moved + grid]
    mul x53 -> x0, local copies, waits for them, and re-layouts: 45.8 us -> none  [the longest x43 42.1 us: tricubic(): total = total + (level_w[above] * row_w[across])[None] * inner]
    pallas_call x0 -> x1, Pallas kernels: none -> 44.4 us  [advect(): pl.pallas_call(functools.partial(advect_kernel, wide, narrow), out_shape=...]
    concatenate x6 -> x0, other arithmetic: 27.3 us -> none  [the longest x4 21.4 us: tricubic(): jnp.concatenate([lowest, lowest, padded, highest, highest], axis=1)]
    ppermute x4, waiting for transfers between devices: 26.3 us -> 0.86 us  [padded_2(): lax.ppermute(lax.slice_in_dim(block, block.shape[dim] - width, None, axis...]
    mul x11 -> x0, other arithmetic: 15.7 us -> none  [the longest x9 13.3 us: tricubic(): total = total + (level_w[above] * row_w[across])[None] * inner]
    concatenate x1, local copies, waits for them, and re-layouts: 0.98 us -> 15.4 us  [advect(): jnp.concatenate([edge, edge, edge, jnp.zeros(edge.shape[:3] + (lanes - 24...]
  transfers between devices with their start and end apart: 10 -> 10, of which waited for: 2 -> 4; matrix products, arithmetic and copies ran while one was open for 52% -> 38% of each run, Pallas kernels for 0% -> 26%
where the time goes in v1:
time: 171 us; the launch traced here: 170 us
  local copies, waits for them, and re-layouts  61.4 us (36%)
  Pallas kernels  44.4 us (26%)
  starting transfers between devices  29.6 us (17%)
  other arithmetic  15.2 us (9%)
  waiting for transfers between devices  14.5 us (8%)
  matrix products  4.62 us (3%)
    pallas_call x1, Pallas kernels, advect(): pl.pallas_call(functools.partial(advect_kernel, wide, narrow), out_shape=...  44.4 us
    unnamed x34, local copies, waits for them, and re-layouts  19.3 us
    concatenate x1, local copies, waits for them, and re-layouts, advect(): jnp.concatenate([edge, edge, edge, jnp.zeros(edge.shape[:3] + (lanes - 24...  15.4 us
    ppermute x4, waiting for transfers between devices, padded_2(): lax.ppermute(lax.slice_in_dim(block, 0, width, axis=dim), axis, backward)  13.6 us
    ppermute x4, starting transfers between devices, padded_2(): lax.ppermute(lax.slice_in_dim(block, 0, width, axis=dim), axis, backward)  9.39 us
    ppermute x4, starting transfers between devices, padded_2(): lax.ppermute(lax.slice_in_dim(block, block.shape[dim] - width, None, axis...  8.26 us
    gather x2, local copies, waits for them, and re-layouts, body(): outgoing = jnp.take(remapped, source_item, axis=0)  7.62 us
    all_to_all x1, starting transfers between devices, body(): lax.all_to_all(marks, ('lat', 'lon'), split_axis=0, concat_axis=0, tiled=...  6.02 us
  transfers between devices with their start and end apart: 10, of which 4 were waited for; matrix products, arithmetic and copies ran while one was open for 38% of the time, Pallas kernels for 26%

profile of v1, /device:TPU:10, one launch (start us, length us, event | category | flops | bytes accessed | tf_op | source)
XLA Modules:
  0.0 169.9 jit_solution(3098959114623376895)
XLA Ops:
  4.0 6.0 %all-to-all-start = ((s32[32,1,2]{2,1,0:T(1,128)}), s32[32,1,2]{2,1,0:T(1,128)S(1)}, u32[]{:S(2)}, u32[]{:S(2)}) async-start(s32[32,1,2]{2,1,0:T(1,128)} %bitcast.8), calls=%async_computation | async-start | bytes 32768 | tf_op jit(solution)/shard_map/all_to_all | solution.py:269
  10.3 3.4 %convolution_convert_fusion = bf16[12,4,128,128]{3,2,1,0:T(8,128)(2,1)} fusion(bf16[12,4,256,128]{3,2,1,0:T(8,128)(2,1)S(1)} %copy-done, bf16[12,128,256]{2,1,0:T(8,128)(2,1)} %param.12), kind=kOutput, calls=%fused_computation.7 | convolution fusion | flops 403439616 | bytes 5505024 | tf_op jit(solution)/shard_map/trc,tkcb->tkrb/dot_general | solution.py:242
  13.6 3.6 %gather_fusion.1 = bf16[64,128,128]{1,2,0:T(8,128)(2,1)} fusion(bf16[48,128,128]{1,2,0:T(8,128)(2,1)} %bitcast.48, s32[1024]{0:T(1024)S(1)} %pad_clamp_fusion), kind=kCustom, calls=%fused_computation.1 | custom fusion | bytes 4194560 | tf_op jit(solution)/shard_map/jit(_take)/gather | solution.py:262
  17.2 4.1 %copy.73 = bf16[64,128,128]{2,1,0:T(8,128)(2,1)} copy(bf16[64,128,128]{1,2,0:T(8,128)(2,1)} %gather_fusion.1) | data formatting | bytes 4194304 | tf_op jit(solution)/shard_map/jit(_take)/gather | solution.py:262
  21.3 3.3 %select_select_fusion = bf16[32,2,128,128]{3,2,1,0:T(8,128)(2,1)} fusion(bf16[32,2,128,128]{3,2,1,0:T(8,128)(2,1)} %bitcast.49, pred[32,2]{1,0:T(8,128)(4,1)S(1)} %compare_and_fusion, pred[32,2]{1,0:T(8,128)(4,1)S(1)} %broadcast_in_dim.50), kind=kLoop, calls=%fused_computation.6 | loop fusion | flops 2097152 | bytes 4194432 | tf_op jit(solution)/shard_map/jit(_where)/select_n | solution.py:263
  24.5 5.9 %all-to-all-start.1 = ((bf16[32,2,128,128]{3,2,1,0:T(8,128)(2,1)}), bf16[32,2,128,128]{3,2,1,0:T(8,128)(2,1)}, u32[]{:S(2)}, u32[]{:S(2)}) async-start(bf16[32,2,128,128]{3,2,1,0:T(8,128)(2,1)} %select_select_fusion), calls=%async_computation.1 | async-start | bytes 4194304 | tf_op jit(solution)/shard_map/all_to_all | solution.py:268
  31.8 1.7 fusion.10
  33.5 2.7 %copy.81 = f32[16,8,16,3]{2,1,3,0:T(8,128)} copy(f32[16,8,16,3]{3,2,1,0:T(8,128)} %get-tuple-element.10) | data formatting | bytes 49152
  36.2 1.5 collective-permute-start.5
  37.8 2.7 %copy.80 = f32[16,8,16,3]{2,1,3,0:T(8,128)} copy(f32[16,8,16,3]{3,2,1,0:T(8,128)} %get-tuple-element.9) | data formatting | bytes 49152
  41.2 2.8 %copy.67 = f32[16,8,16,128]{3,0,2,1:T(8,128)} copy(f32[16,8,16,128]{3,2,1,0:T(8,128)} %param.8) | data formatting | bytes 2097152 | tf_op args[0]
  44.0 3.7 %collective-permute-done.1 = f32[3,8,16,4]{3,1,2,0:T(8,128)S(1)} collective-permute-done((f32[3,8,16,4]{3,1,2,0:T(8,128)}, f32[3,8,16,4]{3,1,2,0:T(8,128)S(1)}, u32[]{:S(2)}, u32[]{:S(2)}) %collective-permute-start.1) | collective-permute-done | bytes 6176 | tf_op jit(solution)/shard_map/ppermute | solution.py:26
  48.6 1.6 pad_maximum_fusion.5
  50.3 3.4 %collective-permute-start.3 = (f32[3,8,4,136]{3,1,2,0:T(8,128)}, f32[3,8,4,136]{3,1,2,0:T(8,128)}, u32[]{:S(2)}, u32[]{:S(2)}) collective-permute-start(f32[3,8,4,136]{3,1,2,0:T(8,128)} %get-tuple-element.12), channel_id=1, source_target_pairs={{8,0},{16,8},{24,16},{9,1},{17,9},{25,17},{10,2},{18,10},{26,18},{... | collective-permute-start | bytes 156680 | tf_op jit(solution)/shard_map/ppermute | solution.py:26
  53.7 3.8 %collective-permute-start.2 = (f32[3,8,4,136]{3,1,2,0:T(8,128)}, f32[3,8,4,136]{3,1,2,0:T(8,128)}, u32[]{:S(2)}, u32[]{:S(2)}) collective-permute-start(f32[3,8,4,136]{3,1,2,0:T(8,128)} %get-tuple-element.11), channel_id=1, source_target_pairs={{0,8},{8,16},{16,24},{1,9},{9,17},{17,25},{2,10},{10,18},{18,26},{... | collective-permute-start | bytes 156680 | tf_op jit(solution)/shard_map/ppermute | solution.py:23
  57.5 2.7 %copy.68 = f32[16,8,16,3]{3,0,2,1:T(8,128)} copy(f32[16,8,16,3]{2,1,3,0:T(8,128)} %collective-permute-done.5) | data formatting | bytes 49152 | tf_op jit(solution)/shard_map/ppermute | solution.py:26
  60.2 2.7 %copy.66 = f32[16,8,16,3]{3,0,2,1:T(8,128)} copy(f32[16,8,16,3]{2,1,3,0:T(8,128)} %collective-permute-done.4) | data formatting | bytes 49152 | tf_op jit(solution)/shard_map/ppermute | solution.py:23
  63.0 2.6 %pad_maximum_fusion.2 = (f32[16,8,3,134]{3,0,2,1:T(8,128)}, f32[16,8,3,134]{3,0,2,1:T(8,128)}) fusion(f32[16,8,16,3]{3,0,2,1:T(8,128)} %copy.68, f32[16,8,16,128]{3,0,2,1:T(8,128)} %copy.67, f32[16,8,16,3]{3,0,2,1:T(8,128)} %copy.66), kind=kLoop, calls=%fused_computation.13 | loop fusion | flops 205824 | bytes 1509376 | tf_op jit(solution)/shard_map/slice | solution.py:24
  65.6 4.1 %collective-permute-start.7 = (f32[16,8,3,134]{3,0,2,1:T(8,128)}, f32[16,8,3,134]{3,0,2,1:T(8,128)}, u32[]{:S(2)}, u32[]{:S(2)}) collective-permute-start(f32[16,8,3,134]{3,0,2,1:T(8,128)} %get-tuple-element.6), channel_id=1, source_target_pairs={{8,0},{16,8},{24,16},{9,1},{17,9},{25,17},{10,2},{18,10},{26,18},{... | collective-permute-start | bytes 617480 | tf_op jit(solution)/shard_map/ppermute | solution.py:26
  69.8 3.5 %collective-permute-start.6 = (f32[16,8,3,134]{3,0,2,1:T(8,128)}, f32[16,8,3,134]{3,0,2,1:T(8,128)}, u32[]{:S(2)}, u32[]{:S(2)}) collective-permute-start(f32[16,8,3,134]{3,0,2,1:T(8,128)} %get-tuple-element.5), channel_id=1, source_target_pairs={{0,8},{8,16},{16,24},{1,9},{9,17},{17,25},{2,10},{10,18},{18,26},{... | collective-permute-start | bytes 617480 | tf_op jit(solution)/shard_map/ppermute | solution.py:23
  76.6 4.3 %collective-permute-done.3 = f32[3,8,4,136]{3,1,2,0:T(8,128)} collective-permute-done((f32[3,8,4,136]{3,1,2,0:T(8,128)}, f32[3,8,4,136]{3,1,2,0:T(8,128)}, u32[]{:S(2)}, u32[]{:S(2)}) %collective-permute-start.3) | collective-permute-done | bytes 52256 | tf_op jit(solution)/shard_map/ppermute | solution.py:26
  80.9 2.2 %maximum_bitcast_fusion.1.wpad_ref = f32[3,24,8,136]{3,2,1,0:T(8,128)} fusion(f32[3,8,4,136]{3,1,2,0:T(8,128)} %collective-permute-done.3, f32[3,8,16,4]{3,1,2,0:T(8,128)} %copy-done.9, f32[3,8,16,128]{3,1,2,0:T(8,128)S(1)} %copy.93, f32[3,8,16,4]{3,1,2,0:T(8,128)} %collective-permute-done, f32[3,8,4,136]{3,1,2,0:T(8,128)} %collective-permute-done.2), kind=kLoop, calls=%fused_computation.10 | loop fusion | flops 313344 | bytes 626688 | tf_op jit(solution)/shard_map/transpose | solution.py:196
  83.1 5.7 %collective-permute-done.7 = f32[16,8,3,134]{3,0,2,1:T(8,128)} collective-permute-done((f32[16,8,3,134]{3,0,2,1:T(8,128)}, f32[16,8,3,134]{3,0,2,1:T(8,128)}, u32[]{:S(2)}, u32[]{:S(2)}) %collective-permute-start.7) | collective-permute-done | bytes 205856 | tf_op jit(solution)/shard_map/ppermute | solution.py:26
  88.7 2.7 %maximum_bitcast_fusion = f32[8,22,16,134]{3,2,1,0:T(8,128)S(1)} fusion(f32[16,8,3,134]{3,0,2,1:T(8,128)} %collective-permute-done.7, f32[16,8,16,3]{3,0,2,1:T(8,128)} %copy.68, f32[16,8,16,128]{3,0,2,1:T(8,128)S(1)} %copy-done.8, f32[16,8,16,3]{3,0,2,1:T(8,128)} %copy.66, f32[16,8,3,134]{3,0,2,1:T(8,128)} %collective-permute-done.6), kind=kLoop, calls=%fused_computation.2 | loop fusion | flops 1509376 | bytes 3018752 | tf_op jit(solution)/shard_map/transpose | solution.py:197
  91.4 1.6 slice.50.main_ref
  93.0 2.2 %fusion.9 = (f32[8,22,16,3]{3,2,1,0:T(8,128)}, f32[8,22,16,3]{3,2,1,0:T(8,128)}) fusion(f32[8,22,16,134]{3,2,1,0:T(8,128)S(1)} %maximum_bitcast_fusion), kind=kLoop, calls=%fused_computation.37 | loop fusion | bytes 135168 | tf_op jit(solution)/shard_map/slice | solution.py:199
  95.1 1.3 broadcast_in_dim.45
  97.7 15.4 %concatenate.21.halo_ref = f32[8,22,16,128]{3,2,1,0:T(8,128)} concatenate(f32[8,22,16,1]{3,2,1,0:T(8,128)} %broadcast_in_dim.45, f32[8,22,16,3]{3,2,1,0:T(8,128)} %get-tuple-element.8, f32[8,22,16,3]{3,2,1,0:T(8,128)} %get-tuple-element.7, f32[8,22,16,1]{3,2,1,0:T(8,128)} %broadcast_in_dim.45, f32[8,22,16,1]{3,2,1,0:T(8,128)} %broadcast_in_dim.45, ...), dimensions={3} | concatenate | bytes 2883584 | tf_op jit(solution)/shard_map/concatenate | solution.py:202
  113.2 1.4 copy-done.1
  114.5 1.4 copy-done.2
  117.9 44.4 %advect.1 = f32[8,16,16,128]{3,2,1,0:T(8,128)S(1)} custom-call(f32[3,16,8,128]{3,2,1,0:T(8,128)S(1)} %bitcast.47, s32[3,16,8,128]{3,2,1,0:T(8,128)S(1)} %copy-done.6, s32[3,16,8,128]{3,2,1,0:T(8,128)S(1)} %get-tuple-element.17.second_ref, f32[3,24,8,136]{3,2,1,0:T(8,128)S(1)} %copy-done.5, f32[8,22,16,128]{3,2,1,0:T(8,128)S(1)} %copy-done.1, ...), custom_call_target="tpu_custom_call" | custom-call | flops 10000000000 | bytes 10000000 | tf_op jit(solution)/shard_map/advect/pallas_call | solution.py:206
  163.2 3.0 %copy.92 = bf16[8,8,128,128]{3,1,2,0:T(8,128)(2,1)S(1)} copy(bf16[8,8,128,128]{3,2,1,0:T(8,128)(2,1)} %bitcast.22) | data formatting | bytes 4194304
  (63 shorter events, 18.4 us)
Async XLA Ops:
  0.0 10.2 %copy-start = (bf16[12,4,256,128]{3,2,1,0:T(8,128)(2,1)S(1)}, bf16[12,4,256,128]{3,2,1,0:T(8,128)(2,1)}, u32[]{:S(2)}) copy-start(bf16[12,4,256,128]{3,2,1,0:T(8,128)(2,1)} %param.13) | copy-start | bytes 9437188
  4.0 20.5 %all-to-all-start = ((s32[32,1,2]{2,1,0:T(1,128)}), s32[32,1,2]{2,1,0:T(1,128)S(1)}, u32[]{:S(2)}, u32[]{:S(2)}) async-start(s32[32,1,2]{2,1,0:T(1,128)} %bitcast.8), calls=%async_computation | async-start | bytes 32768 | tf_op jit(solution)/shard_map/all_to_all | solution.py:269
  24.5 5.9 %copy-start.10 = (f32[3,8,16,128]{3,2,1,0:T(8,128)S(1)}, f32[3,8,16,128]{3,2,1,0:T(8,128)}, u32[]{:S(2)}) copy-start(f32[3,8,16,128]{3,2,1,0:T(8,128)} %param.9) | copy-start | bytes 589828
  24.5 138.7 %all-to-all-start.1 = ((bf16[32,2,128,128]{3,2,1,0:T(8,128)(2,1)}), bf16[32,2,128,128]{3,2,1,0:T(8,128)(2,1)}, u32[]{:S(2)}, u32[]{:S(2)}) async-start(bf16[32,2,128,128]{3,2,1,0:T(8,128)(2,1)} %select_select_fusion), calls=%async_computation.1 | async-start | bytes 4194304 | tf_op jit(solution)/shard_map/all_to_all | solution.py:268
  30.4 1.4 copy-start.7
  31.3 16.4 %collective-permute-start.1 = (f32[3,8,16,4]{3,1,2,0:T(8,128)}, f32[3,8,16,4]{3,1,2,0:T(8,128)S(1)}, u32[]{:S(2)}, u32[]{:S(2)}) collective-permute-start(f32[3,8,16,4]{3,1,2,0:T(8,128)} %get-tuple-element.14), channel_id=1, source_target_pairs={{1,0},{2,1},{3,2},{4,3},{5,4},{6,5},{7,6},{0,7},{9,8},{10,9},{11,1... | collective-permute-start | bytes 18440 | tf_op jit(solution)/shard_map/ppermute | solution.py:26
  31.6 17.0 %collective-permute-start = (f32[3,8,16,4]{3,1,2,0:T(8,128)}, f32[3,8,16,4]{3,1,2,0:T(8,128)}, u32[]{:S(2)}, u32[]{:S(2)}) collective-permute-start(f32[3,8,16,4]{3,1,2,0:T(8,128)} %get-tuple-element.13), channel_id=1, source_target_pairs={{0,1},{1,2},{2,3},{3,4},{4,5},{5,6},{6,7},{7,0},{8,9},{9,10},{10,1... | collective-permute-start | bytes 18440 | tf_op jit(solution)/shard_map/ppermute | solution.py:23
  36.2 21.3 %collective-permute-start.5 = (f32[16,8,16,3]{2,1,3,0:T(8,128)}, f32[16,8,16,3]{2,1,3,0:T(8,128)}, u32[]{:S(2)}, u32[]{:S(2)}) collective-permute-start(f32[16,8,16,3]{2,1,3,0:T(8,128)} %copy.81), channel_id=1, source_target_pairs={{1,0},{2,1},{3,2},{4,3},{5,4},{6,5},{7,6},{0,7},{9,8},{10,9},{11,1... | collective-permute-start | bytes 73736 | tf_op jit(solution)/shard_map/ppermute | solution.py:26
  40.5 19.7 %collective-permute-start.4 = (f32[16,8,16,3]{2,1,3,0:T(8,128)}, f32[16,8,16,3]{2,1,3,0:T(8,128)}, u32[]{:S(2)}, u32[]{:S(2)}) collective-permute-start(f32[16,8,16,3]{2,1,3,0:T(8,128)} %copy.80), channel_id=1, source_target_pairs={{0,1},{1,2},{2,3},{3,4},{4,5},{5,6},{6,7},{7,0},{8,9},{9,10},{10,1... | collective-permute-start | bytes 73736 | tf_op jit(solution)/shard_map/ppermute | solution.py:23
  47.8 17.9 %copy-start.9 = (f32[3,8,16,4]{3,1,2,0:T(8,128)}, f32[3,8,16,4]{3,1,2,0:T(8,128)S(1)}, u32[]{:S(2)}) copy-start(f32[3,8,16,4]{3,1,2,0:T(8,128)S(1)} %collective-permute-done.1) | copy-start | bytes 18436
  50.3 30.6 %collective-permute-start.3 = (f32[3,8,4,136]{3,1,2,0:T(8,128)}, f32[3,8,4,136]{3,1,2,0:T(8,128)}, u32[]{:S(2)}, u32[]{:S(2)}) collective-permute-start(f32[3,8,4,136]{3,1,2,0:T(8,128)} %get-tuple-element.12), channel_id=1, source_target_pairs={{8,0},{16,8},{24,16},{9,1},{17,9},{25,17},{10,2},{18,10},{26,18},{... | collective-permute-start | bytes 156680 | tf_op jit(solution)/shard_map/ppermute | solution.py:26
  53.7 27.2 %collective-permute-start.2 = (f32[3,8,4,136]{3,1,2,0:T(8,128)}, f32[3,8,4,136]{3,1,2,0:T(8,128)}, u32[]{:S(2)}, u32[]{:S(2)}) collective-permute-start(f32[3,8,4,136]{3,1,2,0:T(8,128)} %get-tuple-element.11), channel_id=1, source_target_pairs={{0,8},{8,16},{16,24},{1,9},{9,17},{17,25},{2,10},{10,18},{18,26},{... | collective-permute-start | bytes 156680 | tf_op jit(solution)/shard_map/ppermute | solution.py:23
  63.0 10.3 %copy-start.11 = (s32[3,8,16,128]{3,2,1,0:T(8,128)S(1)}, s32[3,8,16,128]{3,2,1,0:T(8,128)}, u32[]{:S(2)}) copy-start(s32[3,8,16,128]{3,2,1,0:T(8,128)} %param.11) | copy-start | bytes 589828
  63.0 10.3 %copy-start.12 = (s32[3,8,16,128]{3,2,1,0:T(8,128)S(1)}, s32[3,8,16,128]{3,2,1,0:T(8,128)}, u32[]{:S(2)}) copy-start(s32[3,8,16,128]{3,2,1,0:T(8,128)} %param.10) | copy-start | bytes 589828
  65.6 23.1 %collective-permute-start.7 = (f32[16,8,3,134]{3,0,2,1:T(8,128)}, f32[16,8,3,134]{3,0,2,1:T(8,128)}, u32[]{:S(2)}, u32[]{:S(2)}) collective-permute-start(f32[16,8,3,134]{3,0,2,1:T(8,128)} %get-tuple-element.6), channel_id=1, source_target_pairs={{8,0},{16,8},{24,16},{9,1},{17,9},{25,17},{10,2},{18,10},{26,18},{... | collective-permute-start | bytes 617480 | tf_op jit(solution)/shard_map/ppermute | solution.py:26
  69.8 19.0 %collective-permute-start.6 = (f32[16,8,3,134]{3,0,2,1:T(8,128)}, f32[16,8,3,134]{3,0,2,1:T(8,128)}, u32[]{:S(2)}, u32[]{:S(2)}) collective-permute-start(f32[16,8,3,134]{3,0,2,1:T(8,128)} %get-tuple-element.5), channel_id=1, source_target_pairs={{0,8},{8,16},{16,24},{1,9},{9,17},{17,25},{2,10},{10,18},{18,26},{... | collective-permute-start | bytes 617480 | tf_op jit(solution)/shard_map/ppermute | solution.py:23
  76.6 12.1 %copy-start.8 = (f32[16,8,16,128]{3,0,2,1:T(8,128)S(1)}, f32[16,8,16,128]{3,0,2,1:T(8,128)}, u32[]{:S(2)}) copy-start(f32[16,8,16,128]{3,0,2,1:T(8,128)} %copy.67) | copy-start | bytes 3145732
  113.2 1.4 copy-start.1
  114.5 1.4 copy-start.2
  115.9 1.1 copy-start.5
  116.9 0.9 copy-start.6
  162.2 1.0 copy-start.3
  166.8 1.2 copy-start.4
